TPU v7x, 32 devices: a whole 2x2x4 slice. The times are simulated.
32 devices in a mesh: replica: 16 (over z, y, x), dom: 2 (over core).
Axes of the slice: x: 2, y: 2, z: 4, core: 2. Of those that a mesh axis runs over, the one named last changes fastest.
Arguments:
- inputs: bfloat16 [2, 384, 8192], P(None, 'replica', 'dom'), may hold values from -6 to 6
- targets: bfloat16 [2, 384, 8192], P(None, 'replica', 'dom'), may hold values from -0.8984375 to 0.8984375
- w_first: float32 [8192, 8192], P('replica', 'dom'), may hold values from -5 to 5
- acc_first: float32 [8192, 8192], P('replica', 'dom'), may hold values from 0.5 to 8
- w_second: float32 [8192, 8192], P('dom', 'replica'), may hold values from -5 to 5
- acc_second: float32 [8192, 8192], P('dom', 'replica'), may hold values from 0.5 to 8
Outputs:
- new_first: float32 [8192, 8192], P('replica', 'dom')
- new_acc_first: float32 [8192, 8192], P('replica', 'dom')
- new_second: float32 [8192, 8192], P('dom', 'replica')
- new_acc_second: float32 [8192, 8192], P('dom', 'replica')
All inputs are finite; a program needn't handle non-finite values.
Results may differ from a plain program's by a relative error of at most 0.015.
Values may be sent and summed in bfloat16 or wider, within the bound.
No kernel may reach another device: no remote copies, remote signals or barrier semaphores. Data moves between devices by JAX's collectives and lax.ppermute only.
A program may use at most 192 MiB of HBM per device.

v0:
```python
import math
import jax
import jax.numpy as jnp
from jax import lax
from jax.sharding import PartitionSpec as P

learn_rate = 0.05
error_weight = 0.25


def local(inputs, targets, w_first, acc_first, w_second, acc_second):
    full_width = w_first.shape[1] * lax.axis_size("dom")
    unit_scale = 1.0 / math.sqrt(0.4 * full_width)
    for round_index in range(inputs.shape[0]):
        first_half = w_first.astype(jnp.bfloat16)
        second_half = w_second.astype(jnp.bfloat16)
        round_batch = lax.all_gather(inputs[round_index], "replica", axis=0, tiled=True)
        goal_rows = targets[round_index]
        first_terms = (
            lax.dot_general(
                round_batch,
                first_half,
                (((1,), (1,)), ((), ())),
                preferred_element_type=jnp.float32,
            )
            * unit_scale
        )
        first_out = jnp.tanh(lax.psum(first_terms.astype(jnp.bfloat16), "dom").astype(jnp.float32))
        first_rows = first_out.astype(jnp.bfloat16)
        second_out = jnp.tanh(
            lax.psum_scatter(
                lax.dot_general(
                    first_rows,
                    second_half,
                    (((1,), (1,)), ((), ())),
                    preferred_element_type=jnp.float32,
                )
                * unit_scale,
                "replica",
                scatter_dimension=0,
                tiled=True,
            )
        )
        error_own = (
            (second_out - goal_rows.astype(jnp.float32))
            * error_weight
            * (1.0 - second_out * second_out)
        ).astype(jnp.bfloat16)
        error_half = lax.all_gather(error_own, "replica", axis=0, tiled=True)
        second_grad = lax.dot_general(
            error_half, first_rows, (((0,), (0,)), ((), ())), preferred_element_type=jnp.float32
        )
        back_terms = (
            jnp.dot(error_half, second_half, preferred_element_type=jnp.float32) * unit_scale
        )
        back_pre = lax.psum(back_terms.astype(jnp.bfloat16), "dom").astype(jnp.float32)
        first_error = (back_pre * (1.0 - first_out * first_out)).astype(jnp.bfloat16)
        first_grad = lax.dot_general(
            first_error, round_batch, (((0,), (0,)), ((), ())), preferred_element_type=jnp.float32
        )
        acc_first = acc_first + first_grad * first_grad
        w_first = w_first - learn_rate * first_grad / jnp.sqrt(acc_first)
        acc_second = acc_second + second_grad * second_grad
        w_second = w_second - learn_rate * second_grad / jnp.sqrt(acc_second)
    return (w_first, acc_first, w_second, acc_second)


def solution(mesh):
    placed = (
        P(None, "replica", "dom"),
        P(None, "replica", "dom"),
        P("replica", "dom"),
        P("replica", "dom"),
        P("dom", "replica"),
        P("dom", "replica"),
    )
    return jax.shard_map(
        local,
        mesh=mesh,
        in_specs=placed,
        out_specs=(
            P("replica", "dom"),
            P("replica", "dom"),
            P("dom", "replica"),
            P("dom", "replica"),
        ),
        check_vma=False,
    )
```

profile of v0, /device:TPU:0, one launch (start us, length us, event | category | flops | bytes accessed | tf_op | source)
XLA Modules:
  0.0 729.3 jit_solution(1402167555871297250)
XLA Ops:
  7.2 1.8 fusion.71
  9.0 0.0 all-reduce.5.cloned.1.call-start
  9.1 73.1 %all-gather.11.cloned.1.call-done = bf16[1,384,4096]{2,1,0:T(8,128)(2,1)} async-done(((bf16[1,24,4096]{2,1,0:T(8,128)(2,1)}), bf16[1,384,4096]{2,1,0:T(8,128)(2,1)}) %all-gather.11.cloned.1.call-update) | async-done | bytes 3145744 | tf_op jit(solution)/shard_map/all_gather | solution.py:17
  82.2 6.9 fusion.37
  89.2 0.0 reduce-scatter.3.cloned.1.call-start
  89.2 17.1 %all-reduce.5.cloned.1.call-done = bf16[384,512]{1,0:T(8,128)(2,1)} async-done(((bf16[384,512]{1,0:T(8,128)(2,1)}), bf16[384,512]{1,0:T(8,128)(2,1)}) %all-reduce.5.cloned.1.call-update) | async-done | bytes 393232 | tf_op jit(solution)/shard_map/psum | solution.py:28
  106.3 8.1 %convolution_multiply_fusion.1 = f32[384,4096]{1,0:T(8,128)} fusion(f32[4096,512]{1,0:T(8,128)} %param.10, bf16[384,512]{1,0:T(8,128)(2,1)} %all-reduce.5.cloned.1.call-done), kind=kOutput, calls=%fused_computation.9 | convolution fusion | flops 1614675968 | bytes 15073280 | tf_op jit(solution)/shard_map/dot_general | solution.py:32
  114.4 0.0 all-gather.7.cloned.1.call-start
  114.4 147.1 %reduce-scatter.3.cloned.1.call-done = f32[24,4096]{1,0:T(8,128)} async-done(((f32[384,4096]{1,0:T(8,128)}), f32[24,4096]{1,0:T(8,128)}) %reduce-scatter.3.cloned.1.call-update) | async-done | bytes 393232 | tf_op jit(solution)/shard_map/reduce_scatter | solution.py:31
  261.5 1.8 fusion.60
  263.4 0.0 all-reduce.7.cloned.1.call-start
  263.4 69.0 %all-gather.7.cloned.1.call-done = bf16[384,4096]{1,0:T(8,128)(2,1)} async-done(((bf16[24,4096]{1,0:T(8,128)(2,1)}), bf16[384,4096]{1,0:T(8,128)(2,1)}) %all-gather.7.cloned.1.call-update) | async-done | bytes 3145744 | tf_op jit(solution)/shard_map/all_gather | solution.py:49
  332.4 6.9 fusion.45
  339.3 0.0 all-gather.13.cloned.1.call-start
  339.3 0.5 all-gather.13.cloned.1.call-update
  339.9 16.5 %all-reduce.7.cloned.1.call-done = bf16[384,512]{1,0:T(8,128)(2,1)} async-done(((bf16[384,512]{1,0:T(8,128)(2,1)}), bf16[384,512]{1,0:T(8,128)(2,1)}) %all-reduce.7.cloned.1.call-update) | async-done | bytes 393232 | tf_op jit(solution)/shard_map/psum | solution.py:56
  356.4 6.8 fusion.7
  363.2 65.8 %all-gather.13.cloned.1.call-done = bf16[1,384,4096]{2,1,0:T(8,128)(2,1)} async-done(((bf16[1,24,4096]{2,1,0:T(8,128)(2,1)}), bf16[1,384,4096]{2,1,0:T(8,128)(2,1)}) %all-gather.13.cloned.1.call-update) | async-done | bytes 3145744 | tf_op jit(solution)/shard_map/all_gather | solution.py:17
  429.0 12.2 %fusion.48 = bf16[384,512]{1,0:T(8,128)(2,1)} fusion(bf16[1,384,4096]{2,1,0:T(8,128)(2,1)} %all-gather.13.cloned.1.call-done, f32[512,4096]{1,0:T(8,128)} %param.8, f32[512,4096]{1,0:T(8,128)} %fusion.7, f32[512,4096]{1,0:T(8,128)} %param.9), kind=kOutput, calls=%fused_computation.34 | convolution fusion | flops 1623588864 | bytes 28704768 | tf_op jit(solution)/shard_map/dot_general | solution.py:20
  441.2 0.2 reduce-scatter.5.cloned.1.call-start
  441.4 11.2 %multiply_subtract_fusion.2 = (f32[4096,512]{1,0:T(8,128)}, f32[4096,512]{1,0:T(8,128)}) fusion(f32[4096,512]{1,0:T(8,128)} %param.10, f32[4096,512]{1,0:T(8,128)} %param.11, bf16[384,4096]{1,0:T(8,128)(2,1)S(1)} %copy-done.1, bf16[384,512]{1,0:T(8,128)(2,1)S(1)} %copy-done.4), kind=kOutput, calls=%fused_computation.4 | convolution fusion | flops 1621491712 | bytes 37093376 | tf_op jit(solution)/shard_map/dot_general | solution.py:50
  452.6 5.7 all-reduce.9.cloned.1.call-done
  458.3 8.1 %convolution_multiply_fusion = f32[384,4096]{1,0:T(8,128)} fusion(f32[4096,512]{1,0:T(8,128)} %get-tuple-element.10, bf16[384,512]{1,0:T(8,128)(2,1)} %all-reduce.9.cloned.1.call-done), kind=kOutput, calls=%fused_computation.8 | convolution fusion | flops 1614675968 | bytes 15073280 | tf_op jit(solution)/shard_map/dot_general | solution.py:32
  466.5 0.0 all-gather.9.cloned.1.call-start
  466.5 146.6 %reduce-scatter.5.cloned.1.call-done = f32[24,4096]{1,0:T(8,128)} async-done(((f32[384,4096]{1,0:T(8,128)}), f32[24,4096]{1,0:T(8,128)}) %reduce-scatter.5.cloned.1.call-update) | async-done | bytes 393232 | tf_op jit(solution)/shard_map/reduce_scatter | solution.py:31
  613.1 1.8 fusion.57
  614.9 0.0 all-reduce.11.cloned.1.call-start
  615.0 69.2 %all-gather.9.cloned.1.call-done = bf16[384,4096]{1,0:T(8,128)(2,1)} async-done(((bf16[24,4096]{1,0:T(8,128)(2,1)}), bf16[384,4096]{1,0:T(8,128)(2,1)}) %all-gather.9.cloned.1.call-update) | async-done | bytes 3145744 | tf_op jit(solution)/shard_map/all_gather | solution.py:49
  684.2 6.9 fusion.42
  691.1 14.7 %multiply_subtract_fusion = (f32[4096,512]{1,0:T(8,128)}, f32[4096,512]{1,0:T(8,128)}) fusion(f32[4096,512]{1,0:T(8,128)} %get-tuple-element.10, f32[4096,512]{1,0:T(8,128)} %param.11, f32[4096,512]{1,0:T(8,128)} %get-tuple-element.11, bf16[384,4096]{1,0:T(8,128)(2,1)} %all-gather.9.cloned.1.call-done, bf16[384,512]{1,0:T(8,128)(2,1)S(1)} %copy-done.3), kind=kOutput, calls=%fused_computation | convolution fusion | flops 1625686016 | bytes 45481984 | tf_op jit(solution)/shard_map/dot_general | solution.py:50
  705.8 2.4 all-reduce.11.cloned.1.call-done
  708.2 14.2 %multiply_subtract_fusion.1 = (f32[512,4096]{1,0:T(8,128)}, f32[512,4096]{1,0:T(8,128)}) fusion(f32[512,4096]{1,0:T(8,128)} %param.8, f32[512,4096]{1,0:T(8,128)} %param.9, f32[512,4096]{1,0:T(8,128)} %fusion.7, bf16[1,384,4096]{2,1,0:T(8,128)(2,1)S(1)} %copy-done, bf16[384,512]{1,0:T(8,128)(2,1)} %all-reduce.11.cloned.1.call-done, ...), kind=kOutput, calls=%fused_computation.2 | convolution fusion | flops 1632763904 | bytes 45875200 | tf_op jit(solution)/shard_map/dot_general | solution.py:58
  (23 shorter events, 0.2 us)
Async XLA Ops:
  7.2 75.1 %all-gather.11.cloned.1.call-start = ((), (), s32[]{:S(2)}) async-start(), calls=%async_computation.10 | async-start | bytes 3342336 | tf_op jit(solution)/shard_map/all_gather | solution.py:17
  9.0 97.3 %all-reduce.5.cloned.1.call-start = ((), (), s32[]{:S(2)}) async-start(), calls=%async_computation.2 | async-start | bytes 786432 | tf_op jit(solution)/shard_map/psum | solution.py:28
  89.2 172.4 %reduce-scatter.3.cloned.1.call-start = ((), (), s32[]{:S(2)}) async-start(), calls=%async_computation.3 | async-start | bytes 6684672 | tf_op jit(solution)/shard_map/reduce_scatter | solution.py:31
  114.4 242.1 %copy-start.2 = (bf16[1,384,4096]{2,1,0:T(8,128)(2,1)S(1)}, bf16[1,384,4096]{2,1,0:T(8,128)(2,1)}, u32[]{:S(2)}) copy-start(bf16[1,384,4096]{2,1,0:T(8,128)(2,1)} %all-gather.11.cloned.1.call-done) | copy-start | bytes 9437188
  114.4 242.1 %copy-start.4 = (bf16[384,512]{1,0:T(8,128)(2,1)S(1)}, bf16[384,512]{1,0:T(8,128)(2,1)}, u32[]{:S(2)}) copy-start(bf16[384,512]{1,0:T(8,128)(2,1)} %all-reduce.5.cloned.1.call-done) | copy-start | bytes 1179652
  114.4 218.0 %all-gather.7.cloned.1.call-start = ((), (), s32[]{:S(2)}) async-start(), calls=%async_computation.4 | async-start | bytes 3342336 | tf_op jit(solution)/shard_map/all_gather | solution.py:49
  263.4 93.0 %all-reduce.7.cloned.1.call-start = ((), (), s32[]{:S(2)}) async-start(), calls=%async_computation.5 | async-start | bytes 786432 | tf_op jit(solution)/shard_map/psum | solution.py:56
  339.3 89.7 %all-gather.13.cloned.1.call-start = ((), (), s32[]{:S(2)}) async-start(), calls=%async_computation.11 | async-start | bytes 3342336 | tf_op jit(solution)/shard_map/all_gather | solution.py:17
  339.9 118.5 %all-reduce.9.cloned.1.call-start = ((), (), s32[]{:S(2)}) async-start(), calls=%async_computation.6 | async-start | bytes 786432 | tf_op jit(solution)/shard_map/psum | solution.py:28
  363.2 78.2 %copy-start.1 = (bf16[384,4096]{1,0:T(8,128)(2,1)S(1)}, bf16[384,4096]{1,0:T(8,128)(2,1)}, u32[]{:S(2)}) copy-start(bf16[384,4096]{1,0:T(8,128)(2,1)} %all-gather.7.cloned.1.call-done) | copy-start | bytes 9437188
  441.2 171.9 %reduce-scatter.5.cloned.1.call-start = ((), (), s32[]{:S(2)}) async-start(), calls=%async_computation.7 | async-start | bytes 6684672 | tf_op jit(solution)/shard_map/reduce_scatter | solution.py:31
  458.3 154.8 %copy-start.5 = (bf16[2,24,4096]{2,1,0:T(8,128)(2,1)S(1)}, bf16[2,24,4096]{2,1,0:T(8,128)(2,1)}, u32[]{:S(2)}) copy-start(bf16[2,24,4096]{2,1,0:T(8,128)(2,1)} %param.7) | copy-start | bytes 1179652
  466.4 224.6 %copy-start.3 = (bf16[384,512]{1,0:T(8,128)(2,1)S(1)}, bf16[384,512]{1,0:T(8,128)(2,1)}, u32[]{:S(2)}) copy-start(bf16[384,512]{1,0:T(8,128)(2,1)} %all-reduce.9.cloned.1.call-done) | copy-start | bytes 1179652
  466.5 217.7 %all-gather.9.cloned.1.call-start = ((), (), s32[]{:S(2)}) async-start(), calls=%async_computation.8 | async-start | bytes 3342336 | tf_op jit(solution)/shard_map/all_gather | solution.py:49
  614.9 93.3 %all-reduce.11.cloned.1.call-start = ((), (), s32[]{:S(2)}) async-start(), calls=%async_computation.9 | async-start | bytes 786432 | tf_op jit(solution)/shard_map/psum | solution.py:56
  691.1 17.1 %copy-start = (bf16[1,384,4096]{2,1,0:T(8,128)(2,1)S(1)}, bf16[1,384,4096]{2,1,0:T(8,128)(2,1)}, u32[]{:S(2)}) copy-start(bf16[1,384,4096]{2,1,0:T(8,128)(2,1)} %all-gather.13.cloned.1.call-done) | copy-start | bytes 9437188
Sparse Core Ops, SparseCore 0:
  11.3 70.8 all-gather.10
  89.3 16.9 all-reduce.4
  114.5 146.9 reduce-scatter.2
  265.1 67.2 all-gather.6
  339.4 16.9 all-reduce.6
  359.6 69.3 all-gather.12
  441.3 16.9 all-reduce.8
  466.6 146.4 reduce-scatter.4
  616.8 67.2 all-gather.8
  691.2 16.9 all-reduce.10
where the time goes:
time: 730 us; the launch traced here: 729 us
  waiting for transfers between devices  613 us (84%)
  matrix products  96 us (13%)
  between operations  14.2 us (2%)
    reduce_scatter x2, waiting for transfers between devices, local(): lax.psum_scatter(lax.dot_general(first_rows, second_half, (((1,), (1,)),...  294 us
    all_gather x2, waiting for transfers between devices, local(): lax.all_gather(inputs[round_index], 'replica', axis=0, tiled=True)  139 us
    all_gather x2, waiting for transfers between devices, local(): error_half = lax.all_gather(error_own, 'replica', axis=0, tiled=True)  138 us
    dot_general x2, matrix products, local(): lax.dot_general(error_half, first_rows, (((0,), (0,)), ((), ())), preferr...  25.9 us
    psum x2, waiting for transfers between devices, local(): lax.psum(first_terms.astype(jnp.bfloat16), 'dom').astype(jnp.float32)  22.8 us
    dot_general x2, matrix products, local(): lax.dot_general(first_error, round_batch, (((0,), (0,)), ((), ())), prefe...  21 us
    dot_general x2, matrix products, local(): lax.dot_general(round_batch, first_half, (((1,), (1,)), ((), ())), prefer...  19.1 us
    psum x2, waiting for transfers between devices, local(): lax.psum(back_terms.astype(jnp.bfloat16), 'dom').astype(jnp.float32)  18.9 us
  transfers between devices with their start and end apart: 10, of which 10 were waited for; matrix products, arithmetic and copies ran while one was open for 4% of the time, Pallas kernels for 0%

commit v1 on v0

--- a/solution.py
+++ b/solution.py
@@ -53,7 +53,8 @@
         back_terms = (
             jnp.dot(error_half, second_half, preferred_element_type=jnp.float32) * unit_scale
         )
-        back_pre = lax.psum(back_terms.astype(jnp.bfloat16), "dom").astype(jnp.float32)
+        words_close = lambda base_x: jnp.sum(jax.lax.all_gather(base_x, "dom"), 0)
+        back_pre = words_close(back_terms.astype(jnp.bfloat16)).astype(jnp.float32)
         first_error = (back_pre * (1.0 - first_out * first_out)).astype(jnp.bfloat16)
         first_grad = lax.dot_general(
             first_error, round_batch, (((0,), (0,)), ((), ())), preferred_element_type=jnp.float32

time: 730 us -> 706 us (0.967)
  waiting for transfers between devices: 613 us -> 580 us
    psum x2 -> x0, waiting for transfers between devices: 18.9 us -> none  [local(): lax.psum(back_terms.astype(jnp.bfloat16), 'dom').astype(jnp.float32)]
    all_gather x2, waiting for transfers between devices: 139 us -> 126 us  [local(): lax.all_gather(inputs[round_index], 'replica', axis=0, tiled=True)]
  transfers between devices with their start and end apart: 10 -> 8, of which waited for: 10 -> 8; matrix products, arithmetic and copies ran while one was open for 4% -> 4% of each run, Pallas kernels for 0% -> 0%
where the time goes in v1:
time: 706 us; the launch traced here: 705 us
  waiting for transfers between devices  580 us (82%)
  matrix products  95.6 us (14%)
  between operations  14.2 us (2%)
  other arithmetic  7.88 us (1%)
    reduce_scatter x2, waiting for transfers between devices, local(): lax.psum_scatter(lax.dot_general(first_rows, second_half, (((1,), (1,)),...  294 us
    all_gather x2, waiting for transfers between devices, local(): error_half = lax.all_gather(error_own, 'replica', axis=0, tiled=True)  137 us
    all_gather x2, waiting for transfers between devices, local(): lax.all_gather(inputs[round_index], 'replica', axis=0, tiled=True)  126 us
    dot_general x2, matrix products, local(): lax.dot_general(error_half, first_rows, (((0,), (0,)), ((), ())), preferr...  26.9 us
    psum x2, waiting for transfers between devices, local(): lax.psum(first_terms.astype(jnp.bfloat16), 'dom').astype(jnp.float32)  22.8 us
    dot_general x2, matrix products, local(): lax.dot_general(first_error, round_batch, (((0,), (0,)), ((), ())), prefe...  21 us
    dot_general x2, matrix products, local(): lax.dot_general(round_batch, first_half, (((1,), (1,)), ((), ())), prefer...  19.1 us
    dot_general x2, matrix products, local(): lax.dot_general(first_rows, second_half, (((1,), (1,)), ((), ())), prefer...  16.2 us
  transfers between devices with their start and end apart: 8, of which 8 were waited for; matrix products, arithmetic and copies ran while one was open for 4% of the time, Pallas kernels for 0%

profile of v1, /device:TPU:0, one launch (start us, length us, event | category | flops | bytes accessed | tf_op | source)
XLA Modules:
  0.0 705.4 jit_solution(4661089530813263027)
XLA Ops:
  7.2 1.8 fusion.71
  9.0 0.0 all-reduce.3.cloned.1.call-start
  9.1 73.1 %all-gather.13.cloned.1.call-done = bf16[1,384,4096]{2,1,0:T(8,128)(2,1)} async-done(((bf16[1,24,4096]{2,1,0:T(8,128)(2,1)}), bf16[1,384,4096]{2,1,0:T(8,128)(2,1)}) %all-gather.13.cloned.1.call-update) | async-done | bytes 3145744 | tf_op jit(solution)/shard_map/all_gather | solution.py:17
  82.2 6.9 fusion.37
  89.2 0.0 reduce-scatter.3.cloned.1.call-start
  89.2 17.1 %all-reduce.3.cloned.1.call-done = bf16[384,512]{1,0:T(8,128)(2,1)} async-done(((bf16[384,512]{1,0:T(8,128)(2,1)}), bf16[384,512]{1,0:T(8,128)(2,1)}) %all-reduce.3.cloned.1.call-update) | async-done | bytes 393232 | tf_op jit(solution)/shard_map/psum | solution.py:28
  106.3 8.1 %convolution_multiply_fusion.1 = f32[384,4096]{1,0:T(8,128)} fusion(f32[4096,512]{1,0:T(8,128)} %param.10, bf16[384,512]{1,0:T(8,128)(2,1)} %all-reduce.3.cloned.1.call-done), kind=kOutput, calls=%fused_computation.9 | convolution fusion | flops 1614675968 | bytes 15073280 | tf_op jit(solution)/shard_map/dot_general | solution.py:32
  114.4 0.0 all-gather.9.cloned.1.call-start
  114.5 147.1 %reduce-scatter.3.cloned.1.call-done = f32[24,4096]{1,0:T(8,128)} async-done(((f32[384,4096]{1,0:T(8,128)}), f32[24,4096]{1,0:T(8,128)}) %reduce-scatter.3.cloned.1.call-update) | async-done | bytes 393232 | tf_op jit(solution)/shard_map/reduce_scatter | solution.py:31
  261.5 1.8 fusion.60
  263.4 0.0 all-gather.15.cloned.1.call-start
  263.4 0.5 all-gather.15.cloned.1.call-update
  264.0 68.4 %all-gather.9.cloned.1.call-done = bf16[384,4096]{1,0:T(8,128)(2,1)} async-done(((bf16[24,4096]{1,0:T(8,128)(2,1)}), bf16[384,4096]{1,0:T(8,128)(2,1)}) %all-gather.9.cloned.1.call-update) | async-done | bytes 3145744 | tf_op jit(solution)/shard_map/all_gather | solution.py:49
  332.4 6.1 fusion.45
  338.5 2.5 all-gather.1
  341.0 2.1 reduce_sum.24
  343.2 6.8 fusion.7
  350.0 52.7 %all-gather.15.cloned.1.call-done = bf16[1,384,4096]{2,1,0:T(8,128)(2,1)} async-done(((bf16[1,24,4096]{2,1,0:T(8,128)(2,1)}), bf16[1,384,4096]{2,1,0:T(8,128)(2,1)}) %all-gather.15.cloned.1.call-update) | async-done | bytes 3145744 | tf_op jit(solution)/shard_map/all_gather | solution.py:17
  402.6 12.2 %fusion.48 = bf16[384,512]{1,0:T(8,128)(2,1)} fusion(bf16[1,384,4096]{2,1,0:T(8,128)(2,1)} %all-gather.15.cloned.1.call-done, f32[512,4096]{1,0:T(8,128)} %param.8, f32[512,4096]{1,0:T(8,128)} %fusion.7, f32[512,4096]{1,0:T(8,128)} %param.9), kind=kOutput, calls=%fused_computation.34 | convolution fusion | flops 1623588864 | bytes 28704768 | tf_op jit(solution)/shard_map/dot_general | solution.py:20
  414.8 0.2 reduce-scatter.5.cloned.1.call-start
  415.1 11.2 %multiply_subtract_fusion.2 = (f32[4096,512]{1,0:T(8,128)}, f32[4096,512]{1,0:T(8,128)}) fusion(f32[4096,512]{1,0:T(8,128)} %param.10, f32[4096,512]{1,0:T(8,128)} %param.11, bf16[384,4096]{1,0:T(8,128)(2,1)S(1)} %copy-done.1, bf16[384,512]{1,0:T(8,128)(2,1)S(1)} %copy-done.5), kind=kOutput, calls=%fused_computation.4 | convolution fusion | flops 1621491712 | bytes 37093376 | tf_op jit(solution)/shard_map/dot_general | solution.py:50
  426.3 5.7 all-reduce.5.cloned.1.call-done
  432.0 8.1 %convolution_multiply_fusion = f32[384,4096]{1,0:T(8,128)} fusion(f32[4096,512]{1,0:T(8,128)} %get-tuple-element.10, bf16[384,512]{1,0:T(8,128)(2,1)} %all-reduce.5.cloned.1.call-done), kind=kOutput, calls=%fused_computation.8 | convolution fusion | flops 1614675968 | bytes 15073280 | tf_op jit(solution)/shard_map/dot_general | solution.py:32
  440.1 0.0 all-gather.11.cloned.1.call-start
  440.2 146.9 %reduce-scatter.5.cloned.1.call-done = f32[24,4096]{1,0:T(8,128)} async-done(((f32[384,4096]{1,0:T(8,128)}), f32[24,4096]{1,0:T(8,128)}) %reduce-scatter.5.cloned.1.call-update) | async-done | bytes 393232 | tf_op jit(solution)/shard_map/reduce_scatter | solution.py:31
  587.1 1.8 fusion.57
  588.9 68.8 %all-gather.11.cloned.1.call-done = bf16[384,4096]{1,0:T(8,128)(2,1)} async-done(((bf16[24,4096]{1,0:T(8,128)(2,1)}), bf16[384,4096]{1,0:T(8,128)(2,1)}) %all-gather.11.cloned.1.call-update) | async-done | bytes 3145744 | tf_op jit(solution)/shard_map/all_gather | solution.py:49
  657.7 6.3 fusion.42
  664.0 2.5 all-gather.3
  666.5 2.1 reduce_sum.25
  668.6 15.7 %multiply_subtract_fusion = (f32[4096,512]{1,0:T(8,128)}, f32[4096,512]{1,0:T(8,128)}) fusion(f32[4096,512]{1,0:T(8,128)} %get-tuple-element.10, f32[4096,512]{1,0:T(8,128)} %param.11, f32[4096,512]{1,0:T(8,128)} %get-tuple-element.11, bf16[384,4096]{1,0:T(8,128)(2,1)S(1)} %copy-done.3, bf16[384,512]{1,0:T(8,128)(2,1)S(1)} %copy-done.4), kind=kOutput, calls=%fused_computation | convolution fusion | flops 1625686016 | bytes 45481984 | tf_op jit(solution)/shard_map/dot_general | solution.py:50
  684.3 14.2 %multiply_subtract_fusion.1 = (f32[512,4096]{1,0:T(8,128)}, f32[512,4096]{1,0:T(8,128)}) fusion(f32[512,4096]{1,0:T(8,128)} %param.8, f32[512,4096]{1,0:T(8,128)} %param.9, f32[512,4096]{1,0:T(8,128)} %fusion.7, bf16[1,384,4096]{2,1,0:T(8,128)(2,1)S(1)} %copy-done, bf16[384,512]{1,0:T(8,128)(2,1)S(1)} %copy-done.6, bf16[384,512]{1,0:T(8,128)(2,1)S(1)} %copy-done.4), kind=kOutput, calls=%fused_computation.2 | convolution fusion | flops 1632763904 | bytes 45875200 | tf_op jit(solution)/shard_map/dot_general | solution.py:59
  (25 shorter events, 0.2 us)
Async XLA Ops:
  7.2 75.1 %all-gather.13.cloned.1.call-start = ((), (), s32[]{:S(2)}) async-start(), calls=%async_computation.8 | async-start | bytes 3342336 | tf_op jit(solution)/shard_map/all_gather | solution.py:17
  9.0 97.3 %all-reduce.3.cloned.1.call-start = ((), (), s32[]{:S(2)}) async-start(), calls=%async_computation.2 | async-start | bytes 786432 | tf_op jit(solution)/shard_map/psum | solution.py:28
  89.2 172.4 %reduce-scatter.3.cloned.1.call-start = ((), (), s32[]{:S(2)}) async-start(), calls=%async_computation.3 | async-start | bytes 6684672 | tf_op jit(solution)/shard_map/reduce_scatter | solution.py:31
  114.4 228.8 %copy-start.2 = (bf16[1,384,4096]{2,1,0:T(8,128)(2,1)S(1)}, bf16[1,384,4096]{2,1,0:T(8,128)(2,1)}, u32[]{:S(2)}) copy-start(bf16[1,384,4096]{2,1,0:T(8,128)(2,1)} %all-gather.13.cloned.1.call-done) | copy-start | bytes 9437188
  114.4 228.8 %copy-start.5 = (bf16[384,512]{1,0:T(8,128)(2,1)S(1)}, bf16[384,512]{1,0:T(8,128)(2,1)}, u32[]{:S(2)}) copy-start(bf16[384,512]{1,0:T(8,128)(2,1)} %all-reduce.3.cloned.1.call-done) | copy-start | bytes 1179652
  114.4 218.0 %all-gather.9.cloned.1.call-start = ((), (), s32[]{:S(2)}) async-start(), calls=%async_computation.4 | async-start | bytes 3342336 | tf_op jit(solution)/shard_map/all_gather | solution.py:49
  263.4 139.3 %all-gather.15.cloned.1.call-start = ((), (), s32[]{:S(2)}) async-start(), calls=%async_computation.9 | async-start | bytes 3342336 | tf_op jit(solution)/shard_map/all_gather | solution.py:17
  264.0 168.0 %all-reduce.5.cloned.1.call-start = ((), (), s32[]{:S(2)}) async-start(), calls=%async_computation.5 | async-start | bytes 786432 | tf_op jit(solution)/shard_map/psum | solution.py:28
  350.0 65.1 %copy-start.1 = (bf16[384,4096]{1,0:T(8,128)(2,1)S(1)}, bf16[384,4096]{1,0:T(8,128)(2,1)}, u32[]{:S(2)}) copy-start(bf16[384,4096]{1,0:T(8,128)(2,1)} %all-gather.9.cloned.1.call-done) | copy-start | bytes 9437188
  414.8 172.2 %reduce-scatter.5.cloned.1.call-start = ((), (), s32[]{:S(2)}) async-start(), calls=%async_computation.6 | async-start | bytes 6684672 | tf_op jit(solution)/shard_map/reduce_scatter | solution.py:31
  432.0 155.1 %copy-start.7 = (bf16[2,24,4096]{2,1,0:T(8,128)(2,1)S(1)}, bf16[2,24,4096]{2,1,0:T(8,128)(2,1)}, u32[]{:S(2)}) copy-start(bf16[2,24,4096]{2,1,0:T(8,128)(2,1)} %param.7) | copy-start | bytes 1179652
  440.1 228.5 %copy-start.4 = (bf16[384,512]{1,0:T(8,128)(2,1)S(1)}, bf16[384,512]{1,0:T(8,128)(2,1)}, u32[]{:S(2)}) copy-start(bf16[384,512]{1,0:T(8,128)(2,1)} %all-reduce.5.cloned.1.call-done) | copy-start | bytes 1179652
  440.1 217.6 %all-gather.11.cloned.1.call-start = ((), (), s32[]{:S(2)}) async-start(), calls=%async_computation.7 | async-start | bytes 3342336 | tf_op jit(solution)/shard_map/all_gather | solution.py:49
  657.7 10.9 %copy-start.3 = (bf16[384,4096]{1,0:T(8,128)(2,1)S(1)}, bf16[384,4096]{1,0:T(8,128)(2,1)}, u32[]{:S(2)}) copy-start(bf16[384,4096]{1,0:T(8,128)(2,1)} %all-gather.11.cloned.1.call-done) | copy-start | bytes 9437188
  668.6 15.7 %copy-start = (bf16[1,384,4096]{2,1,0:T(8,128)(2,1)S(1)}, bf16[1,384,4096]{2,1,0:T(8,128)(2,1)}, u32[]{:S(2)}) copy-start(bf16[1,384,4096]{2,1,0:T(8,128)(2,1)} %all-gather.15.cloned.1.call-done) | copy-start | bytes 9437188
  668.6 15.7 %copy-start.6 = (bf16[384,512]{1,0:T(8,128)(2,1)S(1)}, bf16[384,512]{1,0:T(8,128)(2,1)}, u32[]{:S(2)}) copy-start(bf16[384,512]{1,0:T(8,128)(2,1)} %reduce_sum.25) | copy-start | bytes 1179652
Sparse Core Ops, SparseCore 0:
  11.3 70.8 all-gather.12
  89.3 16.9 all-reduce.2
  114.5 146.9 reduce-scatter.2
  265.1 67.2 all-gather.8
  336.0 66.6 all-gather.14
  415.0 16.9 all-reduce.4
  440.2 146.7 reduce-scatter.4
  590.4 67.2 all-gather.10
